TPU v7x, 32 devices: a whole 2x2x4 slice. The times are simulated.
32 devices in a mesh: seq: 16 (over z, x, core), ex: 2 (over y).
Axes of the slice: x: 2, y: 2, z: 4, core: 2. Of those that a mesh axis runs over, the one named last changes fastest.
Arguments:
- acts: bfloat16 [4, 2048, 4096], P('ex', 'seq'), may hold values from -6 to 6
- out_grads: bfloat16 [4, 2048, 5120], P('ex', 'seq'), may hold values from -6 to 6
- lengths: int32 [4], P('ex'), may hold values from 512 to 2048, as said below
- in_tiles: bfloat16 [32, 128, 128], replicated, may hold values from -0.09375 to 0.09375
- in_blocks: int32 [32], replicated, may hold values from 0 to 31, each once
- in_signs: int32 [32, 128], replicated, may hold values 0 or 1
- out_tiles: bfloat16 [40, 128, 64], replicated, may hold values from -0.09375 to 0.09375
- out_blocks: int32 [40], replicated, may hold values from 0 to 39, as said below
- out_signs: int32 [40, 128], replicated, may hold values 0 or 1
- query_grads: bfloat16 [2048, 8192], P('seq', 'ex'), may hold values from -6 to 6
Outputs:
- scores: float32 [4, 2048], P('ex', 'seq')
Inputs may be any that keep to these rules, and one draw needn't show every extreme that they name: `lengths`: every training sequence has at least 512 live positions and some sequence has all 2048. `in_blocks`: a permutation of the 32 input feature blocks. `out_blocks`: the first 32 entries are a permutation of 0 to 31, the last 8 a permutation of 32 to 39.
All inputs are finite; a program needn't handle non-finite values.
Results may differ from a plain program's by a relative error of at most 0.005.
Values may be sent and summed in bfloat16 or wider, within the bound.
A program may use at most 64 MiB of HBM per device.

v0:
```python
import jax
import jax.numpy as jnp
from jax import lax
from jax.sharding import PartitionSpec as P


def place(sketch_tiles, block_ids, sign_bits):
    tile_count = sketch_tiles.shape[0]
    chosen = (block_ids[:, None] == jnp.arange(tile_count, dtype=jnp.int32)[None, :]).astype(
        jnp.float32
    )
    signed = sketch_tiles.astype(jnp.float32) * (2 * sign_bits - 1).astype(jnp.float32)[:, :, None]
    placed = jnp.einsum("bc,bik->cik", chosen, signed, precision=lax.Precision.HIGHEST)
    return placed.reshape(tile_count * sketch_tiles.shape[1], sketch_tiles.shape[2]).astype(
        jnp.bfloat16
    )


def widen(placed, split_at):
    out_cols = placed.shape[1]
    upper = jnp.concatenate([placed[:split_at], jnp.zeros((split_at, out_cols), jnp.bfloat16)], 1)
    lower = jnp.concatenate(
        [jnp.zeros((placed.shape[0] - split_at, out_cols), jnp.bfloat16), placed[split_at:]], 1
    )
    return jnp.concatenate([upper, lower], 0)


def per_device(
    acts,
    out_grads,
    lengths,
    in_tiles,
    in_blocks,
    in_signs,
    out_tiles,
    out_blocks,
    out_signs,
    query_grads,
):
    examples_dev, seq_dev, width = acts.shape
    r_in = place(in_tiles, in_blocks, in_signs)
    r_out = widen(place(out_tiles, out_blocks, out_signs), width)
    offset = lax.axis_index("seq") * seq_dev
    positions = offset + jnp.arange(seq_dev, dtype=jnp.int32)
    live_rows = (positions[None, :] < lengths[:, None]).astype(jnp.float32)
    in_sketched = jnp.dot(
        acts.reshape(examples_dev * seq_dev, width), r_in, preferred_element_type=jnp.float32
    )
    in_sketched = (in_sketched.reshape(examples_dev, seq_dev, -1) * live_rows[:, :, None]).astype(
        jnp.bfloat16
    )
    out_sketched = jnp.dot(
        out_grads.reshape(examples_dev * seq_dev, -1), r_out, preferred_element_type=jnp.float32
    )
    out_sketched = out_sketched.reshape(examples_dev, seq_dev, -1).astype(jnp.bfloat16)
    crossed = jnp.einsum(
        "esa,esc->eac", in_sketched, out_sketched, preferred_element_type=jnp.float32
    )
    in_cols = r_in.shape[1] // 2
    out_cols = r_out.shape[1] // 2
    partial_proj = jnp.stack([crossed[:, :in_cols, :out_cols], crossed[:, in_cols:, out_cols:]], 1)
    partial_proj = partial_proj.reshape(examples_dev, -1) / lengths.astype(jnp.float32)[:, None]
    proj_width = partial_proj.shape[1]
    ex_count = lax.axis_size("ex")
    block_width = proj_width // ex_count
    pieces = partial_proj.reshape(examples_dev, ex_count, block_width)
    moved = lax.all_to_all(pieces, "ex", split_axis=1, concat_axis=0, tiled=True)
    summed = lax.psum(moved, "seq")
    owned = summed.astype(jnp.bfloat16).reshape(examples_dev * ex_count, block_width)
    return lax.psum_scatter(
        lax.dot_general(
            owned, query_grads, (((1,), (1,)), ((), ())), preferred_element_type=jnp.float32
        ),
        "ex",
        scatter_dimension=0,
        tiled=True,
    )


def solution(mesh):
    in_specs = (
        P("ex", "seq", None),
        P("ex", "seq", None),
        P("ex"),
        P(),
        P(),
        P(),
        P(),
        P(),
        P(),
        P("seq", "ex"),
    )
    out_specs = P("ex", "seq")
    return jax.shard_map(
        per_device, mesh=mesh, in_specs=in_specs, out_specs=out_specs, check_vma=False
    )
```

profile of v0, /device:TPU:0, one launch (start us, length us, event | category | flops | bytes accessed | tf_op | source)
XLA Modules:
  0.0 92.1 jit_solution(9811729410962465294)
XLA Ops:
  0.0 0.0 copy-start
  0.0 0.9 add_convert_fusion
  0.9 1.2 %convert_multiply_fusion.1 = f32[40,128,64]{1,2,0:T(8,128)S(1)} fusion(bf16[40,128,64]{1,2,0:T(8,128)(2,1)} %param.16, f32[40,128]{1,0:T(8,128)S(1)} %add_convert_fusion), kind=kLoop, calls=%fused_computation.15 | loop fusion | flops 655360 | bytes 1986560 | tf_op jit(solution)/shard_map/mul | solution.py:12
  2.1 2.3 %convolution_convert_fusion = bf16[40,128,64]{1,0,2:T(8,128)(2,1)S(1)} fusion(f32[40,128,64]{1,2,0:T(8,128)S(1)} %convert_multiply_fusion.1, s32[40]{0:T(128)} %param.17), kind=kOutput, calls=%fused_computation.8 | convolution fusion | flops 157615680 | bytes 1966240 | tf_op jit(solution)/shard_map/bc,bik->cik/dot_general | solution.py:13
  4.5 0.2 copy.39
  4.7 0.0 copy-done
  4.7 0.0 copy-start.1
  4.8 1.0 %fusion.18 = bf16[256,128]{0,1:T(8,128)(2,1)S(1)} fusion(bf16[256,5120]{1,0:T(8,128)(2,1)S(1)} %bitcast.46, bf16[1024,64]{0,1:T(8,128)(2,1)S(1)} %bitcast.54, bf16[4096,64]{0,1:T(8,128)(2,1)S(1)} %bitcast.50), kind=kOutput, calls=%fused_computation.18 | convolution fusion | flops 340819968 | bytes 3342336 | tf_op jit(solution)/shard_map/dot_general | solution.py:52
  5.8 0.0 copy-start.3
  5.8 0.1 copy.25
  5.9 0.0 copy-done.1
  5.9 1.8 %convert_multiply_fusion = f32[32,128,128]{2,1,0:T(8,128)S(1)} fusion(bf16[32,128,128]{2,1,0:T(8,128)(2,1)} %param.13, f32[32,128]{1,0:T(8,128)S(1)} %add_convert_fusion.1), kind=kLoop, calls=%fused_computation.6 | loop fusion | flops 1048576 | bytes 3162112 | tf_op jit(solution)/shard_map/mul | solution.py:12
  7.7 0.0 copy-done.3
  7.8 0.0 copy-start.2
  7.8 2.4 %fusion.4 = bf16[32,128,128]{2,0,1:T(8,128)(2,1)S(1)} fusion(f32[32,128,128]{2,1,0:T(8,128)S(1)} %convert_multiply_fusion, s32[32]{0:T(128)S(1)} %copy-done.3), kind=kOutput, calls=%fused_computation.7 | convolution fusion | flops 201851904 | bytes 3145856 | tf_op jit(solution)/shard_map/bc,bik->cik/dot_general | solution.py:13
  10.2 1.4 %copy.21 = bf16[32,128,128]{2,1,0:T(8,128)(2,1)} copy(bf16[32,128,128]{2,0,1:T(8,128)(2,1)S(1)} %fusion.4) | data formatting | bytes 2097152 | tf_op jit(solution)/shard_map/convert_element_type | solution.py:14
  11.6 0.0 copy-done.2
  11.6 0.1 compare_convert_fusion
  11.7 0.0 copy-start.4
  11.7 2.7 %convolution_bitcast_fusion = f32[16,2,8,128]{3,2,1,0:T(8,128)S(1)} fusion(bf16[4096,128]{1,0:T(8,128)(2,1)} %bitcast.47, bf16[256,4096]{1,0:T(8,128)(2,1)} %bitcast.48), kind=kOutput, calls=%fused_computation.16 | convolution fusion | flops 268435456 | bytes 3276800 | tf_op jit(solution)/shard_map/dot_general | solution.py:46
  14.4 0.1 fusion.23
  14.6 0.1 fusion.38
  14.7 0.1 stack.10
  14.8 0.1 stack.9
  14.9 0.7 maximum_divide_fusion
  15.6 4.3 %all-to-all-start = ((f32[2,2,4096]{2,0,1:T(2,128)}), f32[2,2,4096]{2,0,1:T(2,128)S(1)}, u32[]{:S(2)}, u32[]{:S(2)}) async-start(f32[2,2,4096]{2,0,1:T(2,128)} %maximum_divide_fusion), calls=%async_computation | async-start | bytes 131072 | tf_op jit(solution)/shard_map/all_to_all | solution.py:67
  19.9 0.0 copy-done.4
  19.9 0.6 dynamic-slice
  21.1 2.9 %all-to-all-done = f32[2,2,4096]{2,0,1:T(2,128)S(1)} async-done(((f32[2,2,4096]{2,0,1:T(2,128)}), f32[2,2,4096]{2,0,1:T(2,128)S(1)}, u32[]{:S(2)}, u32[]{:S(2)}) %all-to-all-start) | async-done | bytes 65568 | tf_op jit(solution)/shard_map/all_to_all | solution.py:67
  24.0 0.1 all_to_all.16
  24.0 60.9 %psum.7 = bf16[4,1,4096]{2,0,1:T(4,128)(2,1)S(1)} all-reduce(f32[4,1,4096]{2,0,1:T(4,128)S(1)} %all_to_all.16), channel_id=1, replica_groups=mesh['seq'=16,'ex'=2] {'seq'}, use_global_device_ids=true, to_apply=%region_0.0 | all-reduce | flops 16384 | bytes 98304 | tf_op jit(solution)/shard_map/psum | solution.py:68
  85.0 1.6 %fusion.26 = f32[4,128]{1,0:T(4,128)S(1)} fusion(bf16[128,4096]{1,0:T(8,128)(2,1)} %param.19, bf16[4,1,4096]{2,0,1:T(4,128)(2,1)S(1)} %psum.7), kind=kOutput, calls=%fused_computation.27 | convolution fusion | flops 4194304 | bytes 1083392 | tf_op jit(solution)/shard_map/dot_general | solution.py:71
  86.6 4.9 %all-reduce.2 = f32[4,128]{1,0:T(4,128)S(1)} all-reduce(f32[4,128]{1,0:T(4,128)S(1)} %fusion.26), channel_id=2, replica_groups=mesh['seq'=16,'ex'=2] {'ex'}, use_global_device_ids=true, to_apply=%region_1.0.clone | all-reduce | flops 512 | bytes 4096
  91.5 0.6 constant_dynamic-slice_fusion
  (6 shorter events, 0.1 us)
Async XLA Ops:
  0.0 4.7 %copy-start = (bf16[2,128,5120]{2,1,0:T(8,128)(2,1)S(1)}, bf16[2,128,5120]{2,1,0:T(8,128)(2,1)}, u32[]{:S(2)}) copy-start(bf16[2,128,5120]{2,1,0:T(8,128)(2,1)} %param.11) | copy-start | bytes 7864324
  4.7 1.1 %copy-start.1 = (s32[32,128]{1,0:T(8,128)S(1)}, s32[32,128]{1,0:T(8,128)}, u32[]{:S(2)}) copy-start(s32[32,128]{1,0:T(8,128)} %param.15) | copy-start | bytes 49156
  5.8 2.0 %copy-start.3 = (s32[32]{0:T(128)S(1)}, s32[32]{0:T(128)}, u32[]{:S(2)}) copy-start(s32[32]{0:T(128)} %param.14) | copy-start | bytes 388
  7.8 3.9 %copy-start.2 = (s32[2]{0:T(128)S(1)}, s32[2]{0:T(128)}, u32[]{:S(2)}) copy-start(s32[2]{0:T(128)} %param.12) | copy-start | bytes 28
  11.7 8.2 %copy-start.4 = (u32[32]{0:T(128)S(1)}, u32[32]{0:T(128)}, u32[]{:S(2)}) copy-start(u32[32]{0:T(128)} %constant.25) | copy-start | bytes 388
  15.6 8.4 %all-to-all-start = ((f32[2,2,4096]{2,0,1:T(2,128)}), f32[2,2,4096]{2,0,1:T(2,128)S(1)}, u32[]{:S(2)}, u32[]{:S(2)}) async-start(f32[2,2,4096]{2,0,1:T(2,128)} %maximum_divide_fusion), calls=%async_computation | async-start | bytes 131072 | tf_op jit(solution)/shard_map/all_to_all | solution.py:67
where the time goes:
time: 92.4 us; the launch traced here: 92.1 us
  blocking collectives  65.9 us (71%)
  matrix products  10.2 us (11%)
  other arithmetic  4.75 us (5%)
  starting transfers between devices  4.26 us (5%)
  local copies, waits for them, and re-layouts  3.29 us (4%)
  waiting for transfers between devices  2.89 us (3%)
    psum x1, blocking collectives, per_device(): summed = lax.psum(moved, 'seq')  60.9 us
    unnamed x1, blocking collectives  4.93 us
    dot_general x2, matrix products, place(): jnp.einsum('bc,bik->cik', chosen, signed, precision=lax.Precision.HIGHEST)  4.72 us
    all_to_all x1, starting transfers between devices, per_device(): lax.all_to_all(pieces, 'ex', split_axis=1, concat_axis=0, tiled=True)  4.26 us
    mul x2, other arithmetic, place(): sketch_tiles.astype(jnp.float32)  3.08 us
    all_to_all x1, waiting for transfers between devices, per_device(): lax.all_to_all(pieces, 'ex', split_axis=1, concat_axis=0, tiled=True)  2.89 us
    dot_general x1, matrix products, per_device(): jnp.dot(acts.reshape(examples_dev * seq_dev, width), r_in, preferred_elem...  2.74 us
  transfers between devices with their start and end apart: 1, of which 1 were waited for; matrix products, arithmetic and copies ran while one was open for 1% of the time, Pallas kernels for 0%

commit v1 on v0

--- a/solution.py
+++ b/solution.py
@@ -65,7 +65,9 @@
     block_width = proj_width // ex_count
     pieces = partial_proj.reshape(examples_dev, ex_count, block_width)
     moved = lax.all_to_all(pieces, "ex", split_axis=1, concat_axis=0, tiled=True)
-    summed = lax.psum(moved, "seq")
+    summed = moved
+    for hop in (1, 2, 4, 8):
+        summed = summed + lax.ppermute(summed, "seq", [(dev, dev ^ hop) for dev in range(16)])
     owned = summed.astype(jnp.bfloat16).reshape(examples_dev * ex_count, block_width)
     return lax.psum_scatter(
         lax.dot_general(

time: 92.4 us -> 45.9 us (0.50)
  blocking collectives: 65.9 us -> 13.1 us
  waiting for transfers between devices: 2.89 us -> 8.04 us
  starting transfers between devices: 4.26 us -> 5.92 us
    psum x1 -> x0, blocking collectives: 60.9 us -> none  [per_device(): summed = lax.psum(moved, 'seq')]
    all_to_all x0 -> x1, blocking collectives: none -> 8.19 us  [per_device(): lax.all_to_all(pieces, 'ex', split_axis=1, concat_axis=0, tiled=True)]
    ppermute x0 -> x4, waiting for transfers between devices: none -> 8.04 us  [per_device(): lax.ppermute(summed, 'seq', [(dev, dev ^ hop) for dev in range(16)])]
    ppermute x0 -> x4, starting transfers between devices: none -> 5.92 us  [per_device(): lax.ppermute(summed, 'seq', [(dev, dev ^ hop) for dev in range(16)])]
    all_to_all x1 -> x0, starting transfers between devices: 4.26 us -> none  [per_device(): lax.all_to_all(pieces, 'ex', split_axis=1, concat_axis=0, tiled=True)]
    all_to_all x1 -> x0, waiting for transfers between devices: 2.89 us -> none  [per_device(): lax.all_to_all(pieces, 'ex', split_axis=1, concat_axis=0, tiled=True)]
  transfers between devices with their start and end apart: 1 -> 4, of which waited for: 1 -> 4; matrix products, arithmetic and copies ran while one was open for 1% -> 1% of each run, Pallas kernels for 0% -> 0%
where the time goes in v1:
time: 45.9 us; the launch traced here: 45.6 us
  blocking collectives  13.1 us (29%)
  matrix products  10.2 us (22%)
  waiting for transfers between devices  8.04 us (18%)
  starting transfers between devices  5.92 us (13%)
  other arithmetic  4.19 us (9%)
  local copies, waits for them, and re-layouts  3.28 us (7%)
  between operations  0.85 us (2%)
    all_to_all x1, blocking collectives, per_device(): lax.all_to_all(pieces, 'ex', split_axis=1, concat_axis=0, tiled=True)  8.19 us
    ppermute x4, waiting for transfers between devices, per_device(): lax.ppermute(summed, 'seq', [(dev, dev ^ hop) for dev in range(16)])  8.04 us
    ppermute x4, starting transfers between devices, per_device(): lax.ppermute(summed, 'seq', [(dev, dev ^ hop) for dev in range(16)])  5.92 us
    unnamed x1, blocking collectives  4.93 us
    dot_general x2, matrix products, place(): jnp.einsum('bc,bik->cik', chosen, signed, precision=lax.Precision.HIGHEST)  4.72 us
    mul x2, other arithmetic, place(): sketch_tiles.astype(jnp.float32)  3.08 us
    dot_general x1, matrix products, per_device(): jnp.dot(acts.reshape(examples_dev * seq_dev, width), r_in, preferred_elem...  2.74 us
    dot_general x1, matrix products, per_device(): lax.dot_general(owned, query_grads, (((1,), (1,)), ((), ())), preferred_e...  1.59 us
  transfers between devices with their start and end apart: 4, of which 4 were waited for; matrix products, arithmetic and copies ran while one was open for 1% of the time, Pallas kernels for 0%

profile of v1, /device:TPU:0, one launch (start us, length us, event | category | flops | bytes accessed | tf_op | source)
XLA Modules:
  0.0 45.6 jit_solution(4581415204456315485)
XLA Ops:
  0.0 0.0 copy-start
  0.0 0.9 %add_convert_fusion.1 = f32[40,128]{1,0:T(8,128)S(1)} fusion(s32[40,128]{1,0:T(8,128)} %param.18), kind=kLoop, calls=%fused_computation.30 | loop fusion | flops 15360 | bytes 40960 | tf_op jit(solution)/shard_map/convert_element_type | solution.py:12
  0.9 1.2 %convert_multiply_fusion.1 = f32[40,128,64]{1,2,0:T(8,128)S(1)} fusion(bf16[40,128,64]{1,2,0:T(8,128)(2,1)} %param.16, f32[40,128]{1,0:T(8,128)S(1)} %add_convert_fusion.1), kind=kLoop, calls=%fused_computation.15 | loop fusion | flops 655360 | bytes 1986560 | tf_op jit(solution)/shard_map/mul | solution.py:12
  2.1 2.3 %convolution_convert_fusion = bf16[40,128,64]{1,0,2:T(8,128)(2,1)S(1)} fusion(f32[40,128,64]{1,2,0:T(8,128)S(1)} %convert_multiply_fusion.1, s32[40]{0:T(128)} %param.17), kind=kOutput, calls=%fused_computation.8 | convolution fusion | flops 157615680 | bytes 1966240 | tf_op jit(solution)/shard_map/bc,bik->cik/dot_general | solution.py:13
  4.5 0.2 copy.39
  4.7 0.0 copy-done
  4.7 0.0 copy-start.1
  4.8 1.0 %fusion.18 = bf16[256,128]{0,1:T(8,128)(2,1)S(1)} fusion(bf16[256,5120]{1,0:T(8,128)(2,1)S(1)} %bitcast.46, bf16[1024,64]{0,1:T(8,128)(2,1)S(1)} %bitcast.54, bf16[4096,64]{0,1:T(8,128)(2,1)S(1)} %bitcast.50), kind=kOutput, calls=%fused_computation.18 | convolution fusion | flops 340819968 | bytes 3342336 | tf_op jit(solution)/shard_map/dot_general | solution.py:52
  5.8 0.0 copy-start.3
  5.8 0.1 copy.25
  5.9 0.0 copy-done.1
  5.9 1.8 %convert_multiply_fusion = f32[32,128,128]{2,1,0:T(8,128)S(1)} fusion(bf16[32,128,128]{2,1,0:T(8,128)(2,1)} %param.13, f32[32,128]{1,0:T(8,128)S(1)} %add_convert_fusion.2), kind=kLoop, calls=%fused_computation.6 | loop fusion | flops 1048576 | bytes 3162112 | tf_op jit(solution)/shard_map/mul | solution.py:12
  7.7 0.0 copy-done.3
  7.8 0.0 copy-start.2
  7.8 2.4 %fusion.4 = bf16[32,128,128]{2,0,1:T(8,128)(2,1)S(1)} fusion(f32[32,128,128]{2,1,0:T(8,128)S(1)} %convert_multiply_fusion, s32[32]{0:T(128)S(1)} %copy-done.3), kind=kOutput, calls=%fused_computation.7 | convolution fusion | flops 201851904 | bytes 3145856 | tf_op jit(solution)/shard_map/bc,bik->cik/dot_general | solution.py:13
  10.2 1.4 %copy.21 = bf16[32,128,128]{2,1,0:T(8,128)(2,1)} copy(bf16[32,128,128]{2,0,1:T(8,128)(2,1)S(1)} %fusion.4) | data formatting | bytes 2097152 | tf_op jit(solution)/shard_map/convert_element_type | solution.py:14
  11.6 0.0 copy-done.2
  11.6 0.1 compare_convert_fusion
  11.7 0.0 copy-start.4
  11.7 2.7 %convolution_bitcast_fusion = f32[16,2,8,128]{3,2,1,0:T(8,128)S(1)} fusion(bf16[4096,128]{1,0:T(8,128)(2,1)} %bitcast.47, bf16[256,4096]{1,0:T(8,128)(2,1)} %bitcast.48), kind=kOutput, calls=%fused_computation.16 | convolution fusion | flops 268435456 | bytes 3276800 | tf_op jit(solution)/shard_map/dot_general | solution.py:46
  14.4 0.1 fusion.23
  14.6 0.1 fusion.38
  14.7 0.1 stack.10
  14.8 0.1 stack.9
  14.9 0.1 maximum_divide_fusion
  15.0 8.2 %all_to_all.18 = f32[2,2,4096]{2,0,1:T(2,128)S(1)} all-to-all(f32[2,2,4096]{2,0,1:T(2,128)S(1)} %maximum_divide_fusion), channel_id=1, replica_groups=mesh['seq'=16,'ex'=2] {'ex'}, dimensions={1} | all-to-all | bytes 131072 | tf_op jit(solution)/shard_map/all_to_all | solution.py:67
  23.2 0.1 all_to_all.16
  23.2 0.1 collective-permute-start
  23.3 1.2 %collective-permute-done = f32[4,1,4096]{2,0,1:T(4,128)S(1)} collective-permute-done((f32[4,1,4096]{2,0,1:T(4,128)S(1)}, f32[4,1,4096]{2,0,1:T(4,128)S(1)}, u32[]{:S(2)}, u32[]{:S(2)}) %collective-permute-start) | collective-permute-done | bytes 65568 | tf_op jit(solution)/shard_map/ppermute | solution.py:70
  24.6 1.6 %collective-permute-start.1 = (f32[4,1,4096]{2,0,1:T(4,128)S(1)}, f32[4,1,4096]{2,0,1:T(4,128)S(1)}, u32[]{:S(2)}, u32[]{:S(2)}) collective-permute-start(f32[4,1,4096]{2,0,1:T(4,128)S(1)} %add.32), channel_id=1, source_target_pairs={{0,4},{2,6},{4,0},{6,2},{8,12},{10,14},{12,8},{14,10},{16,20},{18,... | collective-permute-start | bytes 196616 | tf_op jit(solution)/shard_map/ppermute | solution.py:70
  26.1 2.8 %collective-permute-done.1 = f32[4,1,4096]{2,0,1:T(4,128)S(1)} collective-permute-done((f32[4,1,4096]{2,0,1:T(4,128)S(1)}, f32[4,1,4096]{2,0,1:T(4,128)S(1)}, u32[]{:S(2)}, u32[]{:S(2)}) %collective-permute-start.1) | collective-permute-done | bytes 65568 | tf_op jit(solution)/shard_map/ppermute | solution.py:70
  28.9 1.6 %collective-permute-start.2 = (f32[4,1,4096]{2,0,1:T(4,128)S(1)}, f32[4,1,4096]{2,0,1:T(4,128)S(1)}, u32[]{:S(2)}, u32[]{:S(2)}) collective-permute-start(f32[4,1,4096]{2,0,1:T(4,128)S(1)} %add.33), channel_id=1, source_target_pairs={{0,8},{2,10},{4,12},{6,14},{8,0},{10,2},{12,4},{14,6},{16,24},{18,... | collective-permute-start | bytes 196616 | tf_op jit(solution)/shard_map/ppermute | solution.py:70
  30.6 2.7 %collective-permute-done.2 = f32[4,1,4096]{2,0,1:T(4,128)S(1)} collective-permute-done((f32[4,1,4096]{2,0,1:T(4,128)S(1)}, f32[4,1,4096]{2,0,1:T(4,128)S(1)}, u32[]{:S(2)}, u32[]{:S(2)}) %collective-permute-start.2) | collective-permute-done | bytes 65568 | tf_op jit(solution)/shard_map/ppermute | solution.py:70
  33.3 2.7 %collective-permute-start.3 = (f32[4,1,4096]{2,0,1:T(4,128)S(1)}, f32[4,1,4096]{2,0,1:T(4,128)S(1)}, u32[]{:S(2)}, u32[]{:S(2)}) collective-permute-start(f32[4,1,4096]{2,0,1:T(4,128)S(1)} %add.34), channel_id=1, source_target_pairs={{0,16},{2,18},{4,20},{6,22},{8,24},{10,26},{12,28},{14,30},{16,0},... | collective-permute-start | bytes 196616 | tf_op jit(solution)/shard_map/ppermute | solution.py:70
  35.9 0.0 copy-done.4
  35.9 0.6 %dynamic-slice = u32[1]{0:T(128)} dynamic-slice(u32[32]{0:T(128)S(1)} %copy-done.4, u32[]{:T(128)S(6)} %add.37), dynamic_slice_sizes={1} | dynamic-slice | bytes 12
  37.2 1.3 %collective-permute-done.3 = f32[4,1,4096]{2,0,1:T(4,128)S(1)} collective-permute-done((f32[4,1,4096]{2,0,1:T(4,128)S(1)}, f32[4,1,4096]{2,0,1:T(4,128)S(1)}, u32[]{:S(2)}, u32[]{:S(2)}) %collective-permute-start.3) | collective-permute-done | bytes 65568 | tf_op jit(solution)/shard_map/ppermute | solution.py:70
  38.5 1.6 %fusion.27 = f32[4,128]{1,0:T(4,128)S(1)} fusion(bf16[128,4096]{1,0:T(8,128)(2,1)} %param.19, f32[4,1,4096]{2,0,1:T(4,128)S(1)} %add.34, f32[4,1,4096]{2,0,1:T(4,128)S(1)} %collective-permute-done.3), kind=kOutput, calls=%fused_computation.29 | convolution fusion | flops 4227072 | bytes 1181696 | tf_op jit(solution)/shard_map/dot_general | solution.py:73
  40.1 4.9 %all-reduce.2 = f32[4,128]{1,0:T(4,128)S(1)} all-reduce(f32[4,128]{1,0:T(4,128)S(1)} %fusion.27), channel_id=2, replica_groups=mesh['seq'=16,'ex'=2] {'ex'}, use_global_device_ids=true, to_apply=%region_0.0.clone | all-reduce | flops 512 | bytes 4096
  45.0 0.6 %constant_dynamic-slice_fusion = f32[2,128]{1,0:T(2,128)} fusion(f32[4,128]{1,0:T(4,128)S(1)} %all-reduce.2, u32[]{:T(128)S(6)} %multiply.1), kind=kLoop, calls=%fused_computation.39 | loop fusion | bytes 2052
  (9 shorter events, 0.1 us)
Async XLA Ops:
  0.0 4.7 %copy-start = (bf16[2,128,5120]{2,1,0:T(8,128)(2,1)S(1)}, bf16[2,128,5120]{2,1,0:T(8,128)(2,1)}, u32[]{:S(2)}) copy-start(bf16[2,128,5120]{2,1,0:T(8,128)(2,1)} %param.11) | copy-start | bytes 7864324
  4.7 1.1 %copy-start.1 = (s32[32,128]{1,0:T(8,128)S(1)}, s32[32,128]{1,0:T(8,128)}, u32[]{:S(2)}) copy-start(s32[32,128]{1,0:T(8,128)} %param.15) | copy-start | bytes 49156
  5.8 2.0 %copy-start.3 = (s32[32]{0:T(128)S(1)}, s32[32]{0:T(128)}, u32[]{:S(2)}) copy-start(s32[32]{0:T(128)} %param.14) | copy-start | bytes 388
  7.8 3.8 %copy-start.2 = (s32[2]{0:T(128)S(1)}, s32[2]{0:T(128)}, u32[]{:S(2)}) copy-start(s32[2]{0:T(128)} %param.12) | copy-start | bytes 28
  11.7 24.2 %copy-start.4 = (u32[32]{0:T(128)S(1)}, u32[32]{0:T(128)}, u32[]{:S(2)}) copy-start(u32[32]{0:T(128)} %constant.25) | copy-start | bytes 388
  23.2 1.3 %collective-permute-start = (f32[4,1,4096]{2,0,1:T(4,128)S(1)}, f32[4,1,4096]{2,0,1:T(4,128)S(1)}, u32[]{:S(2)}, u32[]{:S(2)}) collective-permute-start(f32[4,1,4096]{2,0,1:T(4,128)S(1)} %all_to_all.16), channel_id=1, source_target_pairs={{0,2},{2,0},{4,6},{6,4},{8,10},{10,8},{12,14},{14,12},{16,18},{18,... | collective-permute-start | bytes 196616 | tf_op jit(solution)/shard_map/ppermute | solution.py:70
  24.6 4.3 %collective-permute-start.1 = (f32[4,1,4096]{2,0,1:T(4,128)S(1)}, f32[4,1,4096]{2,0,1:T(4,128)S(1)}, u32[]{:S(2)}, u32[]{:S(2)}) collective-permute-start(f32[4,1,4096]{2,0,1:T(4,128)S(1)} %add.32), channel_id=1, source_target_pairs={{0,4},{2,6},{4,0},{6,2},{8,12},{10,14},{12,8},{14,10},{16,20},{18,... | collective-permute-start | bytes 196616 | tf_op jit(solution)/shard_map/ppermute | solution.py:70
  28.9 4.3 %collective-permute-start.2 = (f32[4,1,4096]{2,0,1:T(4,128)S(1)}, f32[4,1,4096]{2,0,1:T(4,128)S(1)}, u32[]{:S(2)}, u32[]{:S(2)}) collective-permute-start(f32[4,1,4096]{2,0,1:T(4,128)S(1)} %add.33), channel_id=1, source_target_pairs={{0,8},{2,10},{4,12},{6,14},{8,0},{10,2},{12,4},{14,6},{16,24},{18,... | collective-permute-start | bytes 196616 | tf_op jit(solution)/shard_map/ppermute | solution.py:70
  33.3 5.2 %collective-permute-start.3 = (f32[4,1,4096]{2,0,1:T(4,128)S(1)}, f32[4,1,4096]{2,0,1:T(4,128)S(1)}, u32[]{:S(2)}, u32[]{:S(2)}) collective-permute-start(f32[4,1,4096]{2,0,1:T(4,128)S(1)} %add.34), channel_id=1, source_target_pairs={{0,16},{2,18},{4,20},{6,22},{8,24},{10,26},{12,28},{14,30},{16,0},... | collective-permute-start | bytes 196616 | tf_op jit(solution)/shard_map/ppermute | solution.py:70
